TPU v7x, 32 devices: a whole 2x2x4 slice. The times are simulated.
32 devices in a mesh: row: 8 (over y, x, core), col: 4 (over z).
Axes of the slice: x: 2, y: 2, z: 4, core: 2. Of those that a mesh axis runs over, the one named last changes fastest.
Arguments:
- start_modes: float32 [32, 131072], P(None, ('row', 'col')), may hold values from -6 to 6
- energies: float32 [131072], P(('row', 'col')), may hold values from -0.5 to 0.5
- coupling: float32 [2048, 20, 4096], P('row', 'col'), may hold values from -0.078125 to 0.078125
- pattern: int32 [2048, 20], P('row', 'col'), may hold values from 0 to 2047, as said below
Outputs:
- filtered: float32 [32, 131072], P(None, ('row', 'col'))
- previous: float32 [32, 131072], P(None, ('row', 'col'))
Inputs may be any that keep to these rules, and one draw needn't show every extreme that they name: In block row i, the 5 entries pattern[i, c * 5] to pattern[i, c * 5 + 4] are distinct block columns j with (j // 64) % 4 == c.
All inputs are finite; a program needn't handle non-finite values.
Results may differ from a plain program's by a relative error of at most 0.0001.
Values sent between devices are 32-bit elements; how exact they have to be, the bound alone decides.
A program may use at most 192 MiB of HBM per device.

v0:
```python
import jax
import jax.numpy as jnp
from jax import lax
from jax.sharding import PartitionSpec as P

BLOCK = 64
DEGREE = 3


def shards(start_modes, energies, coupling, pattern):
    col_count = lax.axis_size("col")
    mode_count, piece_len = start_modes.shape
    per_piece = piece_len // BLOCK
    rows_here, slot_count = pattern.shape
    piece_ids = pattern // per_piece
    places = piece_ids // col_count * per_piece + pattern % per_piece
    block_mats = coupling.reshape(rows_here, slot_count, BLOCK, BLOCK)

    def coupled(gathered, row_count):
        blocks = gathered.reshape(mode_count, -1, BLOCK)
        sub_mats = block_mats
        picked = jnp.take(blocks, places.reshape(-1), axis=1).reshape(
            mode_count, row_count, per_piece, slot_count, BLOCK
        )
        sub_mats = sub_mats.reshape(row_count, per_piece, slot_count, BLOCK, BLOCK)
        result = jnp.einsum("mqksb,qksab->qmka", picked, sub_mats, precision=lax.Precision.HIGHEST)
        return result.reshape(row_count, mode_count, per_piece * BLOCK)

    def operate(vector):
        gathered = lax.all_gather(vector, "row", axis=1, tiled=True)
        shares_row = lax.psum_scatter(
            coupled(gathered, col_count), "col", scatter_dimension=0, tiled=True
        )[0]
        return energies[None, :] * vector + shares_row

    previous = start_modes
    current = operate(start_modes)
    for degree in range(DEGREE - 1):
        upcoming = 2.0 * operate(current) - previous
        previous = current
        current = upcoming
    return (current, previous)


def solution(mesh):
    in_specs = (P(None, ("row", "col")), P(("row", "col")), P("row", "col", None), P("row", "col"))
    out_specs = (P(None, ("row", "col")), P(None, ("row", "col")))
    return jax.shard_map(shards, mesh=mesh, in_specs=in_specs, out_specs=out_specs, check_vma=False)
```

profile of v0, /device:TPU:0, one launch (start us, length us, event | category | flops | bytes accessed | tf_op | source)
XLA Modules:
  0.0 585.5 jit_solution(14820434715844887029)
XLA Ops:
  9.0 33.5 %reshape_reshape.2 = f32[4,64,5,64,64]{4,3,1,0,2:T(8,128)} reshape(f32[256,5,4096]{2,0,1:T(8,128)} %param.8) | data formatting | bytes 41943040 | tf_op jit(solution)/shard_map/reshape;reshape | solution.py:25
  42.5 6.7 %all-gather.4.cloned.1.call-done = f32[32,32768]{1,0:T(8,128)} async-done(((f32[32,4096]{1,0:T(8,128)}), f32[32,32768]{1,0:T(8,128)}) %all-gather.4.cloned.1.call-update) | async-done | bytes 4194320 | tf_op jit(solution)/shard_map/all_gather | solution.py:30
  49.2 7.3 %reshape.42 = f32[32,512,64]{2,1,0:T(8,128)} reshape(f32[32,32768]{1,0:T(8,128)} %all-gather.4.cloned.1.call-done) | data formatting | bytes 8388608 | tf_op jit(solution)/shard_map/reshape | solution.py:20
  56.5 11.5 %copy.13 = f32[32,512,64]{2,0,1:T(8,128)} copy(f32[32,512,64]{2,1,0:T(8,128)} %reshape.42) | data formatting | bytes 8388608 | tf_op jit(solution)/shard_map/reshape | solution.py:20
  68.0 13.0 %gather_fusion = f32[1280,32,64]{2,1,0:T(8,128)} fusion(f32[32,512,64]{2,0,1:T(8,128)} %copy.13, s32[2048]{0:T(1024)S(1)} %pad_clamp_fusion), kind=kCustom, calls=%fused_computation.clone | custom fusion | bytes 20976640 | tf_op jit(solution)/shard_map/jit(_take)/gather | solution.py:22
  81.0 17.1 %broadcast_select_fusion.2 = f32[1280,32,64]{2,1,0:T(8,128)} fusion(f32[1280,32,64]{2,1,0:T(8,128)} %gather_fusion, pred[1280]{0:T(1024)(128)(4,1)S(1)} %compare_and_fusion), kind=kLoop, calls=%fused_computation.11 | loop fusion | flops 2621440 | bytes 20972800 | tf_op jit(solution)/shard_map/jit(_take)/select_n | solution.py:22
  98.1 48.6 %fusion.6 = f32[4,32,64,64]{3,1,2,0:T(8,128)S(1)} fusion(f32[32,4,64,5,64]{4,0,3,2,1:T(8,128)} %bitcast.50, f32[4,64,5,64,64]{4,3,1,0,2:T(8,128)} %reshape_reshape.2), kind=kOutput, calls=%fused_computation.12 | convolution fusion | flops 2013265920 | bytes 33554432 | tf_op jit(solution)/shard_map/mqksb,qksab->qmka/dot_general | solution.py:26
  151.0 4.8 reshape.45
  155.9 43.7 %reduce-scatter.4.cloned.1.call-done = f32[1,32,4096]{2,1,0:T(8,128)} async-done(((f32[4,32,4096]{2,1,0:T(8,128)}), f32[1,32,4096]{2,1,0:T(8,128)}) %reduce-scatter.4.cloned.1.call-update) | async-done | bytes 524304 | tf_op jit(solution)/shard_map/reduce_scatter | solution.py:31
  201.6 36.3 %all-gather.6.cloned.1.call-done = f32[32,32768]{1,0:T(8,128)} async-done(((f32[32,4096]{1,0:T(8,128)}), f32[32,32768]{1,0:T(8,128)}) %all-gather.6.cloned.1.call-update) | async-done | bytes 4194320 | tf_op jit(solution)/shard_map/all_gather | solution.py:30
  237.9 7.3 %reshape.46 = f32[32,512,64]{2,1,0:T(8,128)} reshape(f32[32,32768]{1,0:T(8,128)} %all-gather.6.cloned.1.call-done) | data formatting | bytes 8388608 | tf_op jit(solution)/shard_map/reshape | solution.py:20
  245.2 11.5 %copy.16 = f32[32,512,64]{2,0,1:T(8,128)} copy(f32[32,512,64]{2,1,0:T(8,128)} %reshape.46) | data formatting | bytes 8388608 | tf_op jit(solution)/shard_map/reshape | solution.py:20
  256.7 13.0 %gather_fusion.1 = f32[1280,32,64]{2,1,0:T(8,128)} fusion(f32[32,512,64]{2,0,1:T(8,128)} %copy.16, s32[2048]{0:T(1024)S(1)} %pad_clamp_fusion), kind=kCustom, calls=%fused_computation.1.clone | custom fusion | bytes 20976640 | tf_op jit(solution)/shard_map/jit(_take)/gather | solution.py:22
  269.7 17.1 %broadcast_select_fusion.1 = f32[1280,32,64]{2,1,0:T(8,128)} fusion(f32[1280,32,64]{2,1,0:T(8,128)} %gather_fusion.1, pred[1280]{0:T(1024)(128)(4,1)S(1)} %compare_and_fusion), kind=kLoop, calls=%fused_computation.10 | loop fusion | flops 2621440 | bytes 20972800 | tf_op jit(solution)/shard_map/jit(_take)/select_n | solution.py:22
  286.8 48.5 %fusion.9 = f32[4,32,64,64]{3,1,2,0:T(8,128)S(1)} fusion(f32[32,4,64,5,64]{4,0,3,2,1:T(8,128)} %bitcast.51, f32[4,64,5,64,64]{4,3,1,0,2:T(8,128)} %reshape_reshape.2), kind=kOutput, calls=%fused_computation.13 | convolution fusion | flops 2013265920 | bytes 33554432 | tf_op jit(solution)/shard_map/mqksb,qksab->qmka/dot_general | solution.py:26
  339.7 4.8 reshape.48
  344.5 43.7 %reduce-scatter.6.cloned.1.call-done = f32[1,32,4096]{2,1,0:T(8,128)} async-done(((f32[4,32,4096]{2,1,0:T(8,128)}), f32[1,32,4096]{2,1,0:T(8,128)}) %reduce-scatter.6.cloned.1.call-update) | async-done | bytes 524304 | tf_op jit(solution)/shard_map/reduce_scatter | solution.py:31
  390.3 36.1 %all-gather.8.cloned.1.call-done = f32[32,32768]{1,0:T(8,128)} async-done(((f32[32,4096]{1,0:T(8,128)}), f32[32,32768]{1,0:T(8,128)}) %all-gather.8.cloned.1.call-update) | async-done | bytes 4194320 | tf_op jit(solution)/shard_map/all_gather | solution.py:30
  426.4 7.3 %reshape.49 = f32[32,512,64]{2,1,0:T(8,128)} reshape(f32[32,32768]{1,0:T(8,128)} %all-gather.8.cloned.1.call-done) | data formatting | bytes 8388608 | tf_op jit(solution)/shard_map/reshape | solution.py:20
  433.7 11.5 %copy.19 = f32[32,512,64]{2,0,1:T(8,128)} copy(f32[32,512,64]{2,1,0:T(8,128)} %reshape.49) | data formatting | bytes 8388608 | tf_op jit(solution)/shard_map/reshape | solution.py:20
  445.2 13.0 %gather_fusion.2 = f32[1280,32,64]{2,1,0:T(8,128)} fusion(f32[32,512,64]{2,0,1:T(8,128)} %copy.19, s32[2048]{0:T(1024)S(1)} %pad_clamp_fusion), kind=kCustom, calls=%fused_computation.2.clone | custom fusion | bytes 20976640 | tf_op jit(solution)/shard_map/jit(_take)/gather | solution.py:22
  458.2 17.1 %broadcast_select_fusion = f32[1280,32,64]{2,1,0:T(8,128)} fusion(f32[1280,32,64]{2,1,0:T(8,128)} %gather_fusion.2, pred[1280]{0:T(1024)(128)(4,1)S(1)} %compare_and_fusion), kind=kLoop, calls=%fused_computation.9 | loop fusion | flops 2621440 | bytes 20972800 | tf_op jit(solution)/shard_map/jit(_take)/select_n | solution.py:22
  475.3 48.3 %fusion.12 = f32[4,32,64,64]{3,1,2,0:T(8,128)S(1)} fusion(f32[32,4,64,5,64]{4,0,3,2,1:T(8,128)} %bitcast.49, f32[4,64,5,64,64]{4,3,1,0,2:T(8,128)} %reshape_reshape.2), kind=kOutput, calls=%fused_computation.14 | convolution fusion | flops 2013265920 | bytes 33554432 | tf_op jit(solution)/shard_map/mqksb,qksab->qmka/dot_general | solution.py:26
  532.7 43.8 %reduce-scatter.8.cloned.1.call-done = f32[1,32,4096]{2,1,0:T(8,128)} async-done(((f32[4,32,4096]{2,1,0:T(8,128)}), f32[1,32,4096]{2,1,0:T(8,128)}) %reduce-scatter.8.cloned.1.call-update) | async-done | bytes 524304 | tf_op jit(solution)/shard_map/reduce_scatter | solution.py:31
  (33 shorter events, 25.8 us)
Async XLA Ops:
  7.2 42.1 %all-gather.4.cloned.1.call-start = ((), (), s32[]{:S(2)}) async-start(), calls=%async_computation.3 | async-start | bytes 4718592 | tf_op jit(solution)/shard_map/all_gather | solution.py:30
  7.9 191.7 %reduce-scatter.4.cloned.1.call-start = ((), (), s32[]{:S(2)}) async-start(), calls=%async_computation.4 | async-start | bytes 2621440 | tf_op jit(solution)/shard_map/reduce_scatter | solution.py:31
  98.1 101.5 %copy-start.1 = (f32[32,4096]{1,0:T(8,128)S(1)}, f32[32,4096]{1,0:T(8,128)}, u32[]{:S(2)}) copy-start(f32[32,4096]{1,0:T(8,128)} %param.6) | copy-start | bytes 1572868
  98.1 101.5 %copy-start.3 = (f32[4096]{0:T(1024)S(1)}, f32[4096]{0:T(1024)}, u32[]{:S(2)}) copy-start(f32[4096]{0:T(1024)} %param.7) | copy-start | bytes 49156
  155.8 82.1 %all-gather.6.cloned.1.call-start = ((), (), s32[]{:S(2)}) async-start(), calls=%async_computation.5 | async-start | bytes 4718592 | tf_op jit(solution)/shard_map/all_gather | solution.py:30
  201.5 186.7 %reduce-scatter.6.cloned.1.call-start = ((), (), s32[]{:S(2)}) async-start(), calls=%async_computation.6 | async-start | bytes 2621440 | tf_op jit(solution)/shard_map/reduce_scatter | solution.py:31
  286.8 101.5 %copy-start = (f32[32,4096]{1,0:T(8,128)S(1)}, f32[32,4096]{1,0:T(8,128)}, u32[]{:S(2)}) copy-start(f32[32,4096]{1,0:T(8,128)} %bitcast_add_fusion.2) | copy-start | bytes 1572868
  344.5 81.9 %all-gather.8.cloned.1.call-start = ((), (), s32[]{:S(2)}) async-start(), calls=%async_computation.7 | async-start | bytes 4718592 | tf_op jit(solution)/shard_map/all_gather | solution.py:30
  390.2 186.3 %reduce-scatter.8.cloned.1.call-start = ((), (), s32[]{:S(2)}) async-start(), calls=%async_computation.8 | async-start | bytes 2621440 | tf_op jit(solution)/shard_map/reduce_scatter | solution.py:31
  475.3 101.3 %copy-start.2 = (f32[32,4096]{1,0:T(8,128)S(1)}, f32[32,4096]{1,0:T(8,128)}, u32[]{:S(2)}) copy-start(f32[32,4096]{1,0:T(8,128)} %fusion.18) | copy-start | bytes 1572868
Sparse Core Ops, SparseCore 0:
  9.9 39.2 all-gather.3
  155.9 43.6 reduce-scatter.3
  202.1 35.7 all-gather.5
  344.6 43.6 reduce-scatter.5
  390.6 35.7 all-gather.7
  532.8 43.6 reduce-scatter.7
where the time goes:
time: 595 us; the launch traced here: 586 us
  waiting for transfers between devices  211 us (35%)
  local copies, waits for them, and re-layouts  157 us (26%)
  matrix products  145 us (24%)
  other arithmetic  57.8 us (10%)
  between operations  14.4 us (2%)
    dot_general x3, matrix products, coupled(): jnp.einsum('mqksb,qksab->qmka', picked, sub_mats, precision=lax.Precision...  145 us
    reduce_scatter x3, waiting for transfers between devices, operate(): lax.psum_scatter(coupled(gathered, col_count), 'col', scatter_dimension=0...  131 us
    all_gather x3, waiting for transfers between devices, operate(): gathered = lax.all_gather(vector, 'row', axis=1, tiled=True)  79.1 us
    reshape x6, local copies, waits for them, and re-layouts, coupled(): blocks = gathered.reshape(mode_count, -1, BLOCK)  56.4 us
    select_n x4, other arithmetic, coupled(): jnp.take(blocks, places.reshape(-1), axis=1)  51.3 us
    gather x3, local copies, waits for them, and re-layouts, coupled(): jnp.take(blocks, places.reshape(-1), axis=1)  39 us
    another operation x1, local copies, waits for them, and re-layouts, coupled(): sub_mats = sub_mats.reshape(row_count, per_piece, slot_count, BLOCK, BLOCK)  33.5 us
    reshape x3, local copies, waits for them, and re-layouts, coupled(): return result.reshape(row_count, mode_count, per_piece * BLOCK)  14.3 us
  transfers between devices with their start and end apart: 6, of which 6 were waited for; matrix products, arithmetic and copies ran while one was open for 6% of the time, Pallas kernels for 0%

commit v1 on v0

--- a/solution.py
+++ b/solution.py
@@ -5,6 +5,23 @@
 
 BLOCK = 64
 DEGREE = 3
+
+
+def joined_along(parts, dim):
+    parts = jnp.moveaxis(parts, 0, dim)
+    shape = parts.shape
+    return parts.reshape(*shape[:dim], shape[dim] * shape[dim + 1], *shape[dim + 2 :])
+
+
+def grow_blocks(shard, axis):
+    length, mine = (lax.axis_size(axis), lax.axis_index(axis))
+    pieces, bit = (shard[None], 1)
+    while bit < length:
+        theirs = lax.ppermute(pieces, axis, [(i, i ^ bit) for i in range(length)])
+        low = mine & bit == 0
+        pieces = jnp.concatenate([jnp.where(low, pieces, theirs), jnp.where(low, theirs, pieces)])
+        bit *= 2
+    return pieces
 
 
 def shards(start_modes, energies, coupling, pattern):
@@ -27,7 +44,7 @@
         return result.reshape(row_count, mode_count, per_piece * BLOCK)
 
     def operate(vector):
-        gathered = lax.all_gather(vector, "row", axis=1, tiled=True)
+        gathered = joined_along(grow_blocks(vector, "row"), 1)
         shares_row = lax.psum_scatter(
             coupled(gathered, col_count), "col", scatter_dimension=0, tiled=True
         )[0]

time: 595 us -> 729 us (1.23)
  waiting for transfers between devices: 211 us -> 310 us
  local copies, waits for them, and re-layouts: 157 us -> 173 us
  starting transfers between devices: 0.24 us -> 11.7 us
    ppermute x0 -> x9, waiting for transfers between devices: none -> 179 us  [grow_blocks(): theirs = lax.ppermute(pieces, axis, [(i, i ^ bit) for i in range(length)])]
    all_gather x3 -> x0, waiting for transfers between devices: 79.1 us -> none  [operate(): gathered = lax.all_gather(vector, 'row', axis=1, tiled=True)]
    another operation x0 -> x6, local copies, waits for them, and re-layouts: none -> 58.7 us  [coupled(): blocks = gathered.reshape(mode_count, -1, BLOCK)]
    reshape x6 -> x0, local copies, waits for them, and re-layouts: 56.4 us -> none  [coupled(): blocks = gathered.reshape(mode_count, -1, BLOCK)]
    transpose x0 -> x3, local copies, waits for them, and re-layouts: none -> 13.5 us  [joined_along(): parts = jnp.moveaxis(parts, 0, dim)]
    ppermute x0 -> x9, starting transfers between devices: none -> 11.6 us  [grow_blocks(): theirs = lax.ppermute(pieces, axis, [(i, i ^ bit) for i in range(length)])]
  transfers between devices with their start and end apart: 6 -> 12, of which waited for: 6 -> 12; matrix products, arithmetic and copies ran while one was open for 6% -> 5% of each run, Pallas kernels for 0% -> 0%
where the time goes in v1:
time: 729 us; the launch traced here: 718 us
  waiting for transfers between devices  310 us (43%)
  local copies, waits for them, and re-layouts  173 us (24%)
  matrix products  145 us (20%)
  other arithmetic  64.7 us (9%)
  between operations  14.2 us (2%)
  starting transfers between devices  11.7 us (2%)
    ppermute x9, waiting for transfers between devices, grow_blocks(): theirs = lax.ppermute(pieces, axis, [(i, i ^ bit) for i in range(length)])  179 us
    dot_general x3, matrix products, coupled(): jnp.einsum('mqksb,qksab->qmka', picked, sub_mats, precision=lax.Precision...  145 us
    reduce_scatter x3, waiting for transfers between devices, operate(): lax.psum_scatter(coupled(gathered, col_count), 'col', scatter_dimension=0...  131 us
    another operation x6, local copies, waits for them, and re-layouts, coupled(): blocks = gathered.reshape(mode_count, -1, BLOCK)  58.7 us
    select_n x4, other arithmetic, coupled(): jnp.take(blocks, places.reshape(-1), axis=1)  51.4 us
    gather x3, local copies, waits for them, and re-layouts, coupled(): jnp.take(blocks, places.reshape(-1), axis=1)  38.9 us
    another operation x1, local copies, waits for them, and re-layouts, coupled(): sub_mats = sub_mats.reshape(row_count, per_piece, slot_count, BLOCK, BLOCK)  33.5 us
  transfers between devices with their start and end apart: 12, of which 12 were waited for; matrix products, arithmetic and copies ran while one was open for 5% of the time, Pallas kernels for 0%

profile of v1, /device:TPU:0, one launch (start us, length us, event | category | flops | bytes accessed | tf_op | source)
XLA Modules:
  0.0 717.7 jit_solution(5311188670130811825)
XLA Ops:
  13.6 23.6 %collective-permute-done.1 = f32[2,32,4096]{2,1,0:T(8,128)} collective-permute-done((f32[2,32,4096]{2,1,0:T(8,128)S(1)}, f32[2,32,4096]{2,1,0:T(8,128)}, u32[]{:S(2)}, u32[]{:S(2)}) %collective-permute-start.1) | collective-permute-done | bytes 1048608 | tf_op jit(solution)/shard_map/ppermute | solution.py:20
  42.2 33.5 %reshape_reshape.15 = f32[4,64,5,64,64]{4,3,1,0,2:T(8,128)} reshape(f32[256,5,4096]{2,0,1:T(8,128)} %param.8) | data formatting | bytes 41943040 | tf_op jit(solution)/shard_map/reshape;reshape | solution.py:42
  75.7 11.8 %collective-permute-done.2 = f32[4,32,4096]{2,1,0:T(8,128)} collective-permute-done((f32[4,32,4096]{2,1,0:T(8,128)}, f32[4,32,4096]{2,1,0:T(8,128)}, u32[]{:S(2)}, u32[]{:S(2)}) %collective-permute-start.2) | collective-permute-done | bytes 2097184 | tf_op jit(solution)/shard_map/ppermute | solution.py:20
  102.2 11.5 %copy.11 = f32[32,512,64]{2,0,1:T(8,128)} copy(f32[32,512,64]{2,1,0:T(8,128)} %reshape_reshape.14) | data formatting | bytes 8388608 | tf_op jit(solution)/shard_map/reshape;reshape | solution.py:37
  113.7 13.0 %gather_fusion = f32[1280,32,64]{2,1,0:T(8,128)} fusion(f32[32,512,64]{2,0,1:T(8,128)} %copy.11, s32[2048]{0:T(1024)S(1)} %pad_clamp_fusion), kind=kCustom, calls=%fused_computation.clone | custom fusion | bytes 20976640 | tf_op jit(solution)/shard_map/jit(_take)/gather | solution.py:39
  126.7 17.2 %broadcast_select_fusion.2 = f32[1280,32,64]{2,1,0:T(8,128)} fusion(f32[1280,32,64]{2,1,0:T(8,128)} %gather_fusion, pred[1280]{0:T(1024)(128)(4,1)S(1)} %compare_and_fusion), kind=kLoop, calls=%fused_computation.11 | loop fusion | flops 2621440 | bytes 20972800 | tf_op jit(solution)/shard_map/jit(_take)/select_n | solution.py:39
  143.9 48.1 %fusion.6 = f32[4,32,64,64]{3,1,2,0:T(8,128)S(1)} fusion(f32[32,4,64,5,64]{4,0,3,2,1:T(8,128)} %bitcast.70, f32[4,64,5,64,64]{4,3,1,0,2:T(8,128)} %reshape_reshape.15), kind=kOutput, calls=%fused_computation.15 | convolution fusion | flops 2013265920 | bytes 33554432 | tf_op jit(solution)/shard_map/mqksb,qksab->qmka/dot_general | solution.py:43
  201.3 44.9 %reduce-scatter.4.cloned.1.call-done = f32[1,32,4096]{2,1,0:T(8,128)} async-done(((f32[4,32,4096]{2,1,0:T(8,128)}), f32[1,32,4096]{2,1,0:T(8,128)}) %reduce-scatter.4.cloned.1.call-update) | async-done | bytes 524304 | tf_op jit(solution)/shard_map/reduce_scatter | solution.py:48
  251.1 23.7 %collective-permute-done.4 = f32[2,32,4096]{2,1,0:T(8,128)S(1)} collective-permute-done((f32[2,32,4096]{2,1,0:T(8,128)S(1)}, f32[2,32,4096]{2,1,0:T(8,128)S(1)}, u32[]{:S(2)}, u32[]{:S(2)}) %collective-permute-start.4) | collective-permute-done | bytes 1048608 | tf_op jit(solution)/shard_map/ppermute | solution.py:20
  276.7 45.3 %collective-permute-done.5 = f32[4,32,4096]{2,1,0:T(8,128)S(1)} collective-permute-done((f32[4,32,4096]{2,1,0:T(8,128)S(1)}, f32[4,32,4096]{2,1,0:T(8,128)S(1)}, u32[]{:S(2)}, u32[]{:S(2)}) %collective-permute-start.5) | collective-permute-done | bytes 2097184 | tf_op jit(solution)/shard_map/ppermute | solution.py:20
  327.4 8.2 %reshape_reshape.16 = f32[32,512,64]{2,1,0:T(8,128)} reshape(f32[32,8,4096]{2,1,0:T(8,128)} %copy.14) | data formatting | bytes 8388608 | tf_op jit(solution)/shard_map/reshape;reshape | solution.py:37
  335.6 11.5 %copy.15 = f32[32,512,64]{2,0,1:T(8,128)} copy(f32[32,512,64]{2,1,0:T(8,128)} %reshape_reshape.16) | data formatting | bytes 8388608 | tf_op jit(solution)/shard_map/reshape;reshape | solution.py:37
  347.1 13.0 %gather_fusion.1 = f32[1280,32,64]{2,1,0:T(8,128)} fusion(f32[32,512,64]{2,0,1:T(8,128)} %copy.15, s32[2048]{0:T(1024)S(1)} %pad_clamp_fusion), kind=kCustom, calls=%fused_computation.1.clone | custom fusion | bytes 20976640 | tf_op jit(solution)/shard_map/jit(_take)/gather | solution.py:39
  360.0 17.1 %broadcast_select_fusion.1 = f32[1280,32,64]{2,1,0:T(8,128)} fusion(f32[1280,32,64]{2,1,0:T(8,128)} %gather_fusion.1, pred[1280]{0:T(1024)(128)(4,1)S(1)} %compare_and_fusion), kind=kLoop, calls=%fused_computation.10 | loop fusion | flops 2621440 | bytes 20972800 | tf_op jit(solution)/shard_map/jit(_take)/select_n | solution.py:39
  377.1 48.3 %fusion.9 = f32[4,32,64,64]{3,1,2,0:T(8,128)S(1)} fusion(f32[32,4,64,5,64]{4,0,3,2,1:T(8,128)} %bitcast.71, f32[4,64,5,64,64]{4,3,1,0,2:T(8,128)} %reshape_reshape.15), kind=kOutput, calls=%fused_computation.16 | convolution fusion | flops 2013265920 | bytes 33554432 | tf_op jit(solution)/shard_map/mqksb,qksab->qmka/dot_general | solution.py:43
  434.7 43.0 %reduce-scatter.6.cloned.1.call-done = f32[1,32,4096]{2,1,0:T(8,128)} async-done(((f32[4,32,4096]{2,1,0:T(8,128)}), f32[1,32,4096]{2,1,0:T(8,128)}) %reduce-scatter.6.cloned.1.call-update) | async-done | bytes 524304 | tf_op jit(solution)/shard_map/reduce_scatter | solution.py:48
  482.5 23.7 %collective-permute-done.7 = f32[2,32,4096]{2,1,0:T(8,128)S(1)} collective-permute-done((f32[2,32,4096]{2,1,0:T(8,128)S(1)}, f32[2,32,4096]{2,1,0:T(8,128)S(1)}, u32[]{:S(2)}, u32[]{:S(2)}) %collective-permute-start.7) | collective-permute-done | bytes 1048608 | tf_op jit(solution)/shard_map/ppermute | solution.py:20
  508.1 45.3 %collective-permute-done.8 = f32[4,32,4096]{2,1,0:T(8,128)S(1)} collective-permute-done((f32[4,32,4096]{2,1,0:T(8,128)S(1)}, f32[4,32,4096]{2,1,0:T(8,128)S(1)}, u32[]{:S(2)}, u32[]{:S(2)}) %collective-permute-start.8) | collective-permute-done | bytes 2097184 | tf_op jit(solution)/shard_map/ppermute | solution.py:20
  558.8 8.2 %reshape_reshape.17 = f32[32,512,64]{2,1,0:T(8,128)} reshape(f32[32,8,4096]{2,1,0:T(8,128)} %copy.18) | data formatting | bytes 8388608 | tf_op jit(solution)/shard_map/reshape;reshape | solution.py:37
  567.0 11.5 %copy.19 = f32[32,512,64]{2,0,1:T(8,128)} copy(f32[32,512,64]{2,1,0:T(8,128)} %reshape_reshape.17) | data formatting | bytes 8388608 | tf_op jit(solution)/shard_map/reshape;reshape | solution.py:37
  578.5 13.0 %gather_fusion.2 = f32[1280,32,64]{2,1,0:T(8,128)} fusion(f32[32,512,64]{2,0,1:T(8,128)} %copy.19, s32[2048]{0:T(1024)S(1)} %pad_clamp_fusion), kind=kCustom, calls=%fused_computation.2.clone | custom fusion | bytes 20976640 | tf_op jit(solution)/shard_map/jit(_take)/gather | solution.py:39
  591.5 17.1 %broadcast_select_fusion = f32[1280,32,64]{2,1,0:T(8,128)} fusion(f32[1280,32,64]{2,1,0:T(8,128)} %gather_fusion.2, pred[1280]{0:T(1024)(128)(4,1)S(1)} %compare_and_fusion), kind=kLoop, calls=%fused_computation.9 | loop fusion | flops 2621440 | bytes 20972800 | tf_op jit(solution)/shard_map/jit(_take)/select_n | solution.py:39
  608.5 48.3 %fusion.12 = f32[4,32,64,64]{3,1,2,0:T(8,128)S(1)} fusion(f32[32,4,64,5,64]{4,0,3,2,1:T(8,128)} %bitcast.69, f32[4,64,5,64,64]{4,3,1,0,2:T(8,128)} %reshape_reshape.15), kind=kOutput, calls=%fused_computation.17 | convolution fusion | flops 2013265920 | bytes 33554432 | tf_op jit(solution)/shard_map/mqksb,qksab->qmka/dot_general | solution.py:43
  666.0 43.0 %reduce-scatter.8.cloned.1.call-done = f32[1,32,4096]{2,1,0:T(8,128)} async-done(((f32[4,32,4096]{2,1,0:T(8,128)}), f32[1,32,4096]{2,1,0:T(8,128)}) %reduce-scatter.8.cloned.1.call-update) | async-done | bytes 524304 | tf_op jit(solution)/shard_map/reduce_scatter | solution.py:48
  (65 shorter events, 79.8 us)
Async XLA Ops:
  7.2 239.1 %reduce-scatter.4.cloned.1.call-start = ((), (), s32[]{:S(2)}) async-start(), calls=%async_computation.3 | async-start | bytes 2621440 | tf_op jit(solution)/shard_map/reduce_scatter | solution.py:48
  7.2 2.3 collective-permute-start
  10.7 26.5 %collective-permute-start.1 = (f32[2,32,4096]{2,1,0:T(8,128)S(1)}, f32[2,32,4096]{2,1,0:T(8,128)}, u32[]{:S(2)}, u32[]{:S(2)}) collective-permute-start(f32[2,32,4096]{2,1,0:T(8,128)S(1)} %pad_maximum_fusion.3), channel_id=1, source_target_pairs={{0,8},{4,12},{8,0},{12,4},{16,24},{20,28},{24,16},{28,20},{1,9},{5... | collective-permute-start | bytes 3145736 | tf_op jit(solution)/shard_map/ppermute | solution.py:20
  13.6 28.2 %copy-start.4 = (s32[256,5]{0,1:T(8,128)S(1)}, s32[256,5]{0,1:T(8,128)}, u32[]{:S(2)}) copy-start(s32[256,5]{0,1:T(8,128)} %param.9) | copy-start | bytes 15364
  40.1 47.4 %collective-permute-start.2 = (f32[4,32,4096]{2,1,0:T(8,128)}, f32[4,32,4096]{2,1,0:T(8,128)}, u32[]{:S(2)}, u32[]{:S(2)}) collective-permute-start(f32[4,32,4096]{2,1,0:T(8,128)} %pad_maximum_fusion), channel_id=1, source_target_pairs={{0,16},{4,20},{8,24},{12,28},{16,0},{20,4},{24,8},{28,12},{1,17},{... | collective-permute-start | bytes 6291464 | tf_op jit(solution)/shard_map/ppermute | solution.py:20
  196.4 49.8 %copy-start = (f32[32,4096]{1,0:T(8,128)S(1)}, f32[32,4096]{1,0:T(8,128)}, u32[]{:S(2)}) copy-start(f32[32,4096]{1,0:T(8,128)} %param.6) | copy-start | bytes 1572868
  196.4 49.8 %copy-start.3 = (f32[4096]{0:T(1024)S(1)}, f32[4096]{0:T(1024)}, u32[]{:S(2)}) copy-start(f32[4096]{0:T(1024)} %param.7) | copy-start | bytes 49156
  201.3 276.4 %reduce-scatter.6.cloned.1.call-start = ((), (), s32[]{:S(2)}) async-start(), calls=%async_computation.4 | async-start | bytes 2621440 | tf_op jit(solution)/shard_map/reduce_scatter | solution.py:48
  247.4 2.0 collective-permute-start.3
  249.5 25.3 %collective-permute-start.4 = (f32[2,32,4096]{2,1,0:T(8,128)S(1)}, f32[2,32,4096]{2,1,0:T(8,128)S(1)}, u32[]{:S(2)}, u32[]{:S(2)}) collective-permute-start(f32[2,32,4096]{2,1,0:T(8,128)S(1)} %pad_maximum_fusion.4), channel_id=1, source_target_pairs={{0,8},{4,12},{8,0},{12,4},{16,24},{20,28},{24,16},{28,20},{1,9},{5... | collective-permute-start | bytes 3145736 | tf_op jit(solution)/shard_map/ppermute | solution.py:20
  275.1 46.9 %collective-permute-start.5 = (f32[4,32,4096]{2,1,0:T(8,128)S(1)}, f32[4,32,4096]{2,1,0:T(8,128)S(1)}, u32[]{:S(2)}, u32[]{:S(2)}) collective-permute-start(f32[4,32,4096]{2,1,0:T(8,128)S(1)} %pad_maximum_fusion.1), channel_id=1, source_target_pairs={{0,16},{4,20},{8,24},{12,28},{16,0},{20,4},{24,8},{28,12},{1,17},{... | collective-permute-start | bytes 6291464 | tf_op jit(solution)/shard_map/ppermute | solution.py:20
  429.8 47.9 %copy-start.1 = (f32[1,32,4096]{2,1,0:T(8,128)S(1)}, f32[1,32,4096]{2,1,0:T(8,128)}, u32[]{:S(2)}) copy-start(f32[1,32,4096]{2,1,0:T(8,128)} %reduce-scatter.4.cloned.1.call-done) | copy-start | bytes 1572868
  434.6 274.3 %reduce-scatter.8.cloned.1.call-start = ((), (), s32[]{:S(2)}) async-start(), calls=%async_computation.5 | async-start | bytes 2621440 | tf_op jit(solution)/shard_map/reduce_scatter | solution.py:48
  478.8 230.2 %copy-start.2 = (f32[32,4096]{1,0:T(8,128)}, f32[32,4096]{1,0:T(8,128)S(1)}, u32[]{:S(2)}) copy-start(f32[32,4096]{1,0:T(8,128)S(1)} %fusion.18) | copy-start | bytes 1572868
  478.8 2.0 collective-permute-start.6
  480.9 25.3 %collective-permute-start.7 = (f32[2,32,4096]{2,1,0:T(8,128)S(1)}, f32[2,32,4096]{2,1,0:T(8,128)S(1)}, u32[]{:S(2)}, u32[]{:S(2)}) collective-permute-start(f32[2,32,4096]{2,1,0:T(8,128)S(1)} %pad_maximum_fusion.5), channel_id=1, source_target_pairs={{0,8},{4,12},{8,0},{12,4},{16,24},{20,28},{24,16},{28,20},{1,9},{5... | collective-permute-start | bytes 3145736 | tf_op jit(solution)/shard_map/ppermute | solution.py:20
  506.5 46.9 %collective-permute-start.8 = (f32[4,32,4096]{2,1,0:T(8,128)S(1)}, f32[4,32,4096]{2,1,0:T(8,128)S(1)}, u32[]{:S(2)}, u32[]{:S(2)}) collective-permute-start(f32[4,32,4096]{2,1,0:T(8,128)S(1)} %pad_maximum_fusion.2), channel_id=1, source_target_pairs={{0,16},{4,20},{8,24},{12,28},{16,0},{20,4},{24,8},{28,12},{1,17},{... | collective-permute-start | bytes 6291464 | tf_op jit(solution)/shard_map/ppermute | solution.py:20
Sparse Core Ops, SparseCore 0:
  201.4 44.8 reduce-scatter.3
  434.7 42.8 reduce-scatter.5
  666.1 42.8 reduce-scatter.7
